TPU v7x, 32 devices: a whole 2x2x4 slice. The times are simulated.
32 devices in a mesh: section: 4 (over x, core), ha: 2 (over y), wa: 4 (over z).
Axes of the slice: x: 2, y: 2, z: 4, core: 2. Of those that a mesh axis runs over, the one named last changes fastest.
Arguments:
- queries: bfloat16 [4, 4, 4, 8, 16, 2560], P('section', None, 'ha', 'wa'), may hold values from -28 to 28
- keys_values: bfloat16 [2, 4, 4, 4, 8, 16, 2560], P(None, 'section', None, 'ha', 'wa'), may hold values from -28 to 28
- grad_out: bfloat16 [4, 4, 4, 8, 16, 2560], P('section', None, 'ha', 'wa'), may hold values from -6 to 6
- time_start: int32 [4, 4, 8], P(None, 'ha', 'wa'), may hold values from 0 to 1, as said below
Outputs:
- grad_qkv: bfloat16 [3, 4, 4, 4, 8, 16, 2560], P(None, 'section', None, 'ha', 'wa')
Inputs may be any that keep to these rules, and one draw needn't show every extreme that they name: Each tile's window begins at most two tiles before the tile and never after it: max(0, t - 2) <= time_start[t, h, w] <= min(t, 1) for time index t.
All inputs are finite; a program needn't handle non-finite values.
Results may differ from a plain program's by a relative error of at most 0.012.
Values may be sent and summed in bfloat16 or wider, within the bound.
A program may use at most 192 MiB of HBM per device.

v0:
```python
import functools

import jax
import jax.numpy as jnp
from jax import lax
from jax.experimental import pallas as pl
from jax.experimental.pallas import tpu as pltpu
from jax.sharding import PartitionSpec as P

HEAD_DIM = 128
HEADS_PER_CHUNK = 2
MESH = pl.DeviceIdType.MESH
F32 = jnp.float32
BF16 = jnp.bfloat16

Y_KV, Z_KV, Z_CORNER, Z_PART, Y_PART, OUT_Q, OUT_KV, KINDS = 0, 1, 3, 5, 7, 8, 9, 10


def dot(a, b, contract):
    return lax.dot_general(a, b, ((contract[0], contract[1]), ((), ())), preferred_element_type=F32)


def kernel(sizes, starts, q, kv, go, out, hy, hz, pz_send, pz_recv, py_send, py_recv,
           acc, acc_y, dq, dkv, bias, send_sem, recv_sem):
    n_sec, n_ha, n_wa, chunks, width = sizes
    grid_t, rows, cols, tok, _ = q.shape
    sec, ha, wa = lax.axis_index("section"), lax.axis_index("ha"), lax.axis_index("wa")
    before = lax.rem(sec + n_sec - 1, n_sec)
    after = lax.rem(sec + 1, n_sec)
    other = 1 - ha
    edge = other * (rows - 1)
    has = (wa > 0, wa < n_wa - 1)
    peer = (wa - 1, wa + 1)
    near = (0, cols - 1)
    scale = HEAD_DIM ** (-0.5)

    barrier = pltpu.get_barrier_semaphore()
    pl.semaphore_signal(barrier, inc=1, device_id=(before, ha, wa), device_id_type=MESH)
    pl.semaphore_signal(barrier, inc=1, device_id=(after, ha, wa), device_id_type=MESH)
    pl.semaphore_signal(barrier, inc=1, device_id=(sec, other, wa), device_id_type=MESH)
    for side in (0, 1):
        @pl.when(has[side])
        def _():
            pl.semaphore_signal(barrier, inc=1, device_id=(sec, ha, peer[side]), device_id_type=MESH)
    pl.semaphore_wait(barrier, 3 + jnp.minimum(wa, 1) + jnp.minimum(n_wa - 1 - wa, 1))

    def lanes(c):
        return pl.ds(pl.multiple_of(c * width, width), width)

    def remote(src, dst, sent, arrived, c, device):
        return pltpu.make_async_remote_copy(
            src_ref=src, dst_ref=dst, send_sem=send_sem.at[sent, c], recv_sem=recv_sem.at[arrived, c],
            device_id=device, device_id_type=MESH)

    def y_kv(c):
        return remote(kv.at[:, :, edge, :, :, lanes(c)], hy.at[:, :, :, :, lanes(c)],
                      Y_KV, Y_KV, c, (sec, other, wa))

    def z_kv(side, c):
        return remote(kv.at[:, :, :, near[side], :, lanes(c)], hz.at[1 - side, :, :, 0:rows, :, lanes(c)],
                      Z_KV + side, Z_KV + 1 - side, c, (sec, ha, peer[side]))

    def z_corner(side, c):
        return remote(hy.at[:, :, near[side], :, lanes(c)], hz.at[1 - side, :, :, rows, :, lanes(c)],
                      Z_CORNER + side, Z_CORNER + 1 - side, c, (sec, ha, peer[side]))

    def z_part(side, c):
        return remote(pz_send.at[side, :, :, :, :, lanes(c)], pz_recv.at[1 - side, :, :, :, :, lanes(c)],
                      Z_PART + side, Z_PART + 1 - side, c, (sec, ha, peer[side]))

    def y_part(c):
        return remote(py_send.at[:, :, :, :, lanes(c)], py_recv.at[:, :, :, :, lanes(c)],
                      Y_PART, Y_PART, c, (sec, other, wa))

    def out_q(c):
        return remote(dq.at[:, :, :, :, lanes(c)], out.at[0, :, :, :, :, lanes(c)],
                      OUT_Q, OUT_Q, c, (before, ha, wa))

    def out_kv(c):
        return remote(dkv.at[:, :, :, :, :, lanes(c)], out.at[pl.ds(1, 2), :, :, :, :, lanes(c)],
                      OUT_KV, OUT_KV, c, (before, ha, wa))

    n_own, n_y, n_z = grid_t * rows * cols * tok, grid_t * cols * tok, grid_t * (rows + 1) * tok
    n_q = n_own
    cut = (0, n_own, n_own + n_y, n_own + n_y + n_z, n_own + n_y + 2 * n_z)

    def stage_send(c):
        y_kv(c).start()
        for side in (0, 1):
            @pl.when(has[side])
            def _():
                z_kv(side, c).start()

    def stage_corner(c):
        y_kv(c).wait_recv()
        for side in (0, 1):
            @pl.when(has[side])
            def _():
                z_corner(side, c).start()

    def head(h):
        ch = pl.ds(pl.multiple_of(h * HEAD_DIM, HEAD_DIM), HEAD_DIM)
        qh = q[:, :, :, :, ch].reshape(n_q, HEAD_DIM)
        gh = go[:, :, :, :, ch].reshape(n_q, HEAD_DIM)

        def gather(i):
            return jnp.concatenate([
                kv[i, :, :, :, :, ch].reshape(n_own, HEAD_DIM), hy[i, :, :, :, ch].reshape(n_y, HEAD_DIM),
                hz[0, i, :, :, :, ch].reshape(n_z, HEAD_DIM), hz[1, i, :, :, :, ch].reshape(n_z, HEAD_DIM)])

        k, v = gather(0), gather(1)
        s = dot(k, qh, ((1,), (1,))) * scale + bias[...]
        e = jnp.exp(s - jnp.max(s, axis=0, keepdims=True))
        p = e * (1.0 / jnp.sum(e, axis=0, keepdims=True))
        dp = dot(v, gh, ((1,), (1,)))
        delta = jnp.sum(p * dp, axis=0, keepdims=True)
        ds = (p * (dp - delta)).astype(BF16)
        grads = (dot(ds, qh, ((1,), (0,))) * scale, dot(p.astype(BF16), gh, ((1,), (0,))))
        q_grad = dot(ds, k, ((0,), (0,))) * scale
        dq[:, :, :, :, ch] = q_grad.astype(BF16).reshape(grid_t, rows, cols, tok, HEAD_DIM)
        for i in (0, 1):
            acc[i, :, :, :, :, ch] = grads[i][cut[0]:cut[1]].reshape(grid_t, rows, cols, tok, HEAD_DIM)
            acc_y[i, :, :, :, ch] = grads[i][cut[1]:cut[2]].reshape(grid_t, cols, tok, HEAD_DIM)
            for side in (0, 1):
                part = grads[i][cut[2 + side]:cut[3 + side]].astype(BF16)
                pz_send[side, i, :, :, :, ch] = part.reshape(grid_t, rows + 1, tok, HEAD_DIM)

    def stage_compute(c):
        for side in (0, 1):
            @pl.when(has[side])
            def _():
                arrived_z(side, c)
        for j in range(HEADS_PER_CHUNK):
            head(c * HEADS_PER_CHUNK + j)
        for side in (0, 1):
            @pl.when(has[side])
            def _():
                z_part(side, c).start()
        out_q(c).start()

    def arrived_z(side, c):
        z_kv(1 - side, c).wait_recv()
        z_corner(1 - side, c).wait_recv()

    def stage_fold(c):
        ch = lanes(c)
        for side in (0, 1):
            @pl.when(has[side])
            def _():
                z_part(1 - side, c).wait_recv()
                for i in (0, 1):
                    acc[i, :, :, near[side], :, ch] += pz_recv[side, i, :, 0:rows, :, ch].astype(F32)
                    acc_y[i, :, near[side], :, ch] += pz_recv[side, i, :, rows, :, ch].astype(F32)
        py_send[:, :, :, :, ch] = acc_y[:, :, :, :, ch].astype(BF16)
        y_part(c).start()

    def stage_out(c):
        ch = lanes(c)
        y_part(c).wait_recv()
        acc[:, :, edge, :, :, ch] += py_recv[:, :, :, :, ch].astype(F32)
        dkv[:, :, :, :, :, ch] = acc[:, :, :, :, :, ch].astype(BF16)
        out_kv(c).start()

    stage_send(0)
    stage_send(1)

    lane = lax.broadcasted_iota(jnp.int32, (1, n_q), 1)
    first = jnp.zeros((1, n_q), jnp.int32)
    for t in range(grid_t):
        for r in range(rows):
            for c in range(cols):
                tile = (t * rows + r) * cols + c
                first = jnp.where(lane // tok == tile, starts[t, r, c], first)
    col = (lane // tok) % cols
    low_first, high_last = wa == 0, wa == n_wa - 1
    in_left = jnp.where(low_first, 0, jnp.where(high_last, 1, (col == 0).astype(jnp.int32)))
    in_right = jnp.where(high_last, 0, jnp.where(low_first, 1, (col == cols - 1).astype(jnp.int32)))
    always = jnp.ones((1, n_q), jnp.int32)
    for at, per_t, inside in ((0, rows * cols * tok, always), (1, cols * tok, always),
                              (2, (rows + 1) * tok, in_left), (3, (rows + 1) * tok, in_right)):
        for t in range(grid_t):
            seen = (first <= t) & (first + 2 >= t) & (inside > 0)
            row = jnp.where(seen, 0.0, -1e30).astype(F32)
            bias[cut[at] + t * per_t:cut[at] + (t + 1) * per_t, :] = jnp.broadcast_to(row, (per_t, n_q))
    for side in (0, 1):
        @pl.when(jnp.logical_not(has[side]))
        def _():
            hz[side] = jnp.zeros(hz.shape[1:], BF16)

    def step(i, carry):
        @pl.when(i + 2 < chunks)
        def _():
            stage_send(i + 2)

        @pl.when(i + 1 < chunks)
        def _():
            stage_corner(i + 1)

        @pl.when(i < chunks)
        def _():
            stage_compute(i)

        @pl.when((i >= 1) & (i < chunks + 1))
        def _():
            stage_fold(i - 1)

        @pl.when(i >= 2)
        def _():
            stage_out(i - 2)
        return carry

    stage_corner(0)
    lax.fori_loop(0, chunks + 2, step, 0)

    def finish(c, carry):
        y_kv(c).wait_send()
        y_part(c).wait_send()
        for side in (0, 1):
            @pl.when(has[side])
            def _():
                z_kv(side, c).wait_send()
                z_corner(side, c).wait_send()
                z_part(side, c).wait_send()
        out_q(c).wait()
        out_kv(c).wait()
        return carry

    lax.fori_loop(0, chunks, finish, 0)


def local(mesh_sizes, queries, keys_values, grad_out, time_start):
    n_sec, n_ha, n_wa = mesh_sizes
    q, kv, go = queries[0], keys_values[:, 0], grad_out[0]
    grid_t, rows, cols, tok, channels = q.shape
    assert n_ha == 2 and rows == 2 and cols == 2 and n_wa >= 2 and n_sec >= 2
    width = HEADS_PER_CHUNK * HEAD_DIM
    assert channels % width == 0
    chunks = channels // width
    assert chunks >= 2
    n_q = grid_t * rows * cols * tok
    n_k = n_q + grid_t * tok * (cols + 2 * (rows + 1))
    vmem = pl.BlockSpec(memory_space=pltpu.VMEM)
    out = pl.pallas_call(
        functools.partial(kernel, (n_sec, n_ha, n_wa, chunks, width)),
        out_shape=jax.ShapeDtypeStruct((3,) + q.shape, BF16),
        in_specs=[pl.BlockSpec(memory_space=pltpu.SMEM), vmem, vmem, vmem],
        out_specs=pl.BlockSpec(memory_space=pl.ANY),
        scratch_shapes=[
            pltpu.VMEM((2, grid_t, cols, tok, channels), BF16),
            pltpu.VMEM((2, 2, grid_t, rows + 1, tok, channels), BF16),
            pltpu.VMEM((2, 2, grid_t, rows + 1, tok, channels), BF16),
            pltpu.VMEM((2, 2, grid_t, rows + 1, tok, channels), BF16),
            pltpu.VMEM((2, grid_t, cols, tok, channels), BF16),
            pltpu.VMEM((2, grid_t, cols, tok, channels), BF16),
            pltpu.VMEM((2,) + q.shape, F32),
            pltpu.VMEM((2, grid_t, cols, tok, channels), F32),
            pltpu.VMEM(q.shape, BF16),
            pltpu.VMEM((2,) + q.shape, BF16),
            pltpu.VMEM((n_k, n_q), F32),
            pltpu.SemaphoreType.DMA((KINDS, chunks)),
            pltpu.SemaphoreType.DMA((KINDS, chunks)),
        ],
        compiler_params=pltpu.CompilerParams(
            collective_id=0, has_side_effects=True, vmem_limit_bytes=60 * 1024 * 1024
        ),
    )(time_start, q, kv, go)
    return out[:, None]


def solution(mesh):
    sizes = (mesh.shape["section"], mesh.shape["ha"], mesh.shape["wa"])
    return jax.shard_map(
        functools.partial(local, sizes),
        mesh=mesh,
        in_specs=(
            P("section", None, "ha", "wa", None, None),
            P(None, "section", None, "ha", "wa", None, None),
            P("section", None, "ha", "wa", None, None),
            P(None, "ha", "wa"),
        ),
        out_specs=P(None, "section", None, "ha", "wa", None, None),
        check_vma=False,
    )
```

profile of v0, /device:TPU:1, one launch (start us, length us, event | category | flops | bytes accessed | tf_op | source)
XLA Modules:
  0.0 109.7 jit_solution(8892175991654690225)
XLA Ops:
  0.0 1.4 %copy.5.starts = s32[4,2,2]{2,1,0:T(2,128)} copy(s32[4,2,2]{0,2,1:T(2,128)} %param.7) | data formatting | bytes 128 | tf_op args[3]
  1.4 103.9 %shard_map.46 = bf16[3,4,2,2,16,2560]{5,4,3,2,1,0:T(8,128)(2,1)} custom-call(s32[4,2,2]{2,1,0:T(2,128)} %copy.5.starts, bf16[4,2,2,16,2560]{4,3,2,1,0:T(8,128)(2,1)} %bitcast.8, bf16[2,4,2,2,16,2560]{5,4,3,2,1,0:T(8,128)(2,1)} %bitcast.7, bf16[4,2,2,16,2560]{4,3,2,1,0:T(8,128)(2,1)} %bitcast.9), custom_call_target="tpu_custom_call" | custom-call | tf_op jit(solution)/shard_map/pallas_call | solution.py:243
  105.3 4.4 %copy.8 = bf16[3,1,4,2,2,16,2560]{6,5,4,3,2,1,0:T(8,128)(2,1)} copy(bf16[3,1,4,2,2,16,2560]{6,5,4,3,2,1,0:T(8,128)(2,1)} %bitcast.6) | data formatting | bytes 7864320
where the time goes:
time: 110 us
  Pallas kernels  104 us (95%)
  local copies, waits for them, and re-layouts  5.77 us (5%)
    pallas_call x1, Pallas kernels, local(): pl.pallas_call(functools.partial(kernel, (n_sec, n_ha, n_wa, chunks, widt...  104 us
    unnamed x2, local copies, waits for them, and re-layouts  5.77 us

commit v1 on v0

--- a/solution.py
+++ b/solution.py
@@ -13,14 +13,21 @@
 F32 = jnp.float32
 BF16 = jnp.bfloat16
 
-Y_KV, Z_KV, Z_CORNER, Z_PART, Y_PART, OUT_Q, OUT_KV, KINDS = 0, 1, 3, 5, 7, 8, 9, 10
+Y_KV, Z_KV, CORNER, Z_PART, Y_PART, OUT_Q, OUT_KV, CORNER_PART, KINDS = 0, 1, 3, 5, 7, 8, 9, 10, 12
+
+AHEAD = 2
+CORNERS_AHEAD = 1
+
+
+def wa_first(c):
+    return lax.rem(c, 3) == 2
 
 
 def dot(a, b, contract):
     return lax.dot_general(a, b, ((contract[0], contract[1]), ((), ())), preferred_element_type=F32)
 
 
-def kernel(sizes, starts, q, kv, go, out, hy, hz, pz_send, pz_recv, py_send, py_recv,
+def kernel(sizes, starts, q_in, kv_in, go_in, out, q, kv, go, load_sem, hy, hz, pz_send, pz_recv, py_send, py_recv,
            acc, acc_y, dq, dkv, bias, send_sem, recv_sem):
     n_sec, n_ha, n_wa, chunks, width = sizes
     grid_t, rows, cols, tok, _ = q.shape
@@ -34,6 +41,8 @@
     near = (0, cols - 1)
     scale = HEAD_DIM ** (-0.5)
 
+    loads = [pltpu.make_async_copy(src, dst, load_sem.at[n])
+             for n, (src, dst) in enumerate(((q_in, q), (kv_in, kv), (go_in, go)))]
     barrier = pltpu.get_barrier_semaphore()
     pl.semaphore_signal(barrier, inc=1, device_id=(before, ha, wa), device_id_type=MESH)
     pl.semaphore_signal(barrier, inc=1, device_id=(after, ha, wa), device_id_type=MESH)
@@ -53,20 +62,28 @@
             device_id=device, device_id_type=MESH)
 
     def y_kv(c):
-        return remote(kv.at[:, :, edge, :, :, lanes(c)], hy.at[:, :, :, :, lanes(c)],
+        return remote(kv_in.at[:, :, edge, :, :, lanes(c)], hy.at[:, :, :, :, lanes(c)],
                       Y_KV, Y_KV, c, (sec, other, wa))
 
     def z_kv(side, c):
-        return remote(kv.at[:, :, :, near[side], :, lanes(c)], hz.at[1 - side, :, :, 0:rows, :, lanes(c)],
+        return remote(kv_in.at[:, :, :, near[side], :, lanes(c)], hz.at[1 - side, :, :, 0:rows, :, lanes(c)],
                       Z_KV + side, Z_KV + 1 - side, c, (sec, ha, peer[side]))
 
     def z_corner(side, c):
         return remote(hy.at[:, :, near[side], :, lanes(c)], hz.at[1 - side, :, :, rows, :, lanes(c)],
-                      Z_CORNER + side, Z_CORNER + 1 - side, c, (sec, ha, peer[side]))
-
-    def z_part(side, c):
-        return remote(pz_send.at[side, :, :, :, :, lanes(c)], pz_recv.at[1 - side, :, :, :, :, lanes(c)],
+                      CORNER + side, CORNER + 1 - side, c, (sec, ha, peer[side]))
+
+    def y_corner(side, c):
+        return remote(hz.at[side, :, :, edge, :, lanes(c)], hz.at[side, :, :, rows, :, lanes(c)],
+                      CORNER + side, CORNER + side, c, (sec, other, wa))
+
+    def z_part(side, c, count):
+        return remote(pz_send.at[side, :, :, 0:count, :, lanes(c)], pz_recv.at[1 - side, :, :, 0:count, :, lanes(c)],
                       Z_PART + side, Z_PART + 1 - side, c, (sec, ha, peer[side]))
+
+    def corner_part(side, c):
+        return remote(pz_send.at[side, :, :, rows, :, lanes(c)], pz_recv.at[side, :, :, rows, :, lanes(c)],
+                      CORNER_PART + side, CORNER_PART + side, c, (sec, other, wa))
 
     def y_part(c):
         return remote(py_send.at[:, :, :, :, lanes(c)], py_recv.at[:, :, :, :, lanes(c)],
@@ -91,12 +108,24 @@
             def _():
                 z_kv(side, c).start()
 
-    def stage_corner(c):
-        y_kv(c).wait_recv()
+    def sides(action):
         for side in (0, 1):
             @pl.when(has[side])
             def _():
-                z_corner(side, c).start()
+                action(side)
+
+    def stage_corner(c):
+        def ha_then_wa():
+            y_kv(c).wait_recv()
+            sides(lambda side: z_corner(side, c).start())
+
+        def wa_then_ha():
+            def pass_on(side):
+                z_kv(1 - side, c).wait_recv()
+                y_corner(side, c).start()
+            sides(pass_on)
+
+        lax.cond(wa_first(c), wa_then_ha, ha_then_wa)
 
     def head(h):
         ch = pl.ds(pl.multiple_of(h * HEAD_DIM, HEAD_DIM), HEAD_DIM)
@@ -126,43 +155,76 @@
                 pz_send[side, i, :, :, :, ch] = part.reshape(grid_t, rows + 1, tok, HEAD_DIM)
 
     def stage_compute(c):
-        for side in (0, 1):
-            @pl.when(has[side])
-            def _():
-                arrived_z(side, c)
+        def ha_then_wa():
+            def arrive(side):
+                z_kv(1 - side, c).wait_recv()
+                z_corner(1 - side, c).wait_recv()
+            sides(arrive)
+
+        def wa_then_ha():
+            y_kv(c).wait_recv()
+            sides(lambda side: y_corner(side, c).wait_recv())
+
+        lax.cond(wa_first(c), wa_then_ha, ha_then_wa)
         for j in range(HEADS_PER_CHUNK):
             head(c * HEADS_PER_CHUNK + j)
-        for side in (0, 1):
-            @pl.when(has[side])
-            def _():
-                z_part(side, c).start()
+
+        def send_ha_then_wa():
+            sides(lambda side: z_part(side, c, rows + 1).start())
+
+        def send_wa_then_ha():
+            py_send[:, :, :, :, lanes(c)] = acc_y[:, :, :, :, lanes(c)].astype(BF16)
+            y_part(c).start()
+            sides(lambda side: corner_part(side, c).start())
+
+        lax.cond(wa_first(c), send_wa_then_ha, send_ha_then_wa)
         out_q(c).start()
-
-    def arrived_z(side, c):
-        z_kv(1 - side, c).wait_recv()
-        z_corner(1 - side, c).wait_recv()
 
     def stage_fold(c):
         ch = lanes(c)
-        for side in (0, 1):
-            @pl.when(has[side])
-            def _():
-                z_part(1 - side, c).wait_recv()
+
+        def ha_then_wa():
+            def fold(side):
+                z_part(1 - side, c, rows + 1).wait_recv()
                 for i in (0, 1):
                     acc[i, :, :, near[side], :, ch] += pz_recv[side, i, :, 0:rows, :, ch].astype(F32)
                     acc_y[i, :, near[side], :, ch] += pz_recv[side, i, :, rows, :, ch].astype(F32)
-        py_send[:, :, :, :, ch] = acc_y[:, :, :, :, ch].astype(BF16)
-        y_part(c).start()
+            sides(fold)
+            py_send[:, :, :, :, ch] = acc_y[:, :, :, :, ch].astype(BF16)
+            y_part(c).start()
+
+        def wa_then_ha():
+            def fold(side):
+                corner_part(side, c).wait_recv()
+                for i in (0, 1):
+                    pz_send[side, i, :, edge, :, ch] = (
+                        pz_send[side, i, :, edge, :, ch].astype(F32) + pz_recv[side, i, :, rows, :, ch].astype(F32)
+                    ).astype(BF16)
+                z_part(side, c, rows).start()
+            sides(fold)
+
+        lax.cond(wa_first(c), wa_then_ha, ha_then_wa)
 
     def stage_out(c):
         ch = lanes(c)
         y_part(c).wait_recv()
         acc[:, :, edge, :, :, ch] += py_recv[:, :, :, :, ch].astype(F32)
+
+        @pl.when(wa_first(c))
+        def _():
+            def fold(side):
+                z_part(1 - side, c, rows).wait_recv()
+                for i in (0, 1):
+                    acc[i, :, :, near[side], :, ch] += pz_recv[side, i, :, 0:rows, :, ch].astype(F32)
+            sides(fold)
+
         dkv[:, :, :, :, :, ch] = acc[:, :, :, :, :, ch].astype(BF16)
         out_kv(c).start()
 
-    stage_send(0)
-    stage_send(1)
+    for c in range(AHEAD):
+        stage_send(c)
+    for load in loads:
+        load.start()
 
     lane = lax.broadcasted_iota(jnp.int32, (1, n_q), 1)
     first = jnp.zeros((1, n_q), jnp.int32)
@@ -170,7 +232,7 @@
         for r in range(rows):
             for c in range(cols):
                 tile = (t * rows + r) * cols + c
-                first = jnp.where(lane // tok == tile, starts[t, r, c], first)
+                first = jnp.where(lane // tok == tile, starts[r, c, t], first)
     col = (lane // tok) % cols
     low_first, high_last = wa == 0, wa == n_wa - 1
     in_left = jnp.where(low_first, 0, jnp.where(high_last, 1, (col == 0).astype(jnp.int32)))
@@ -188,13 +250,13 @@
             hz[side] = jnp.zeros(hz.shape[1:], BF16)
 
     def step(i, carry):
-        @pl.when(i + 2 < chunks)
-        def _():
-            stage_send(i + 2)
-
-        @pl.when(i + 1 < chunks)
-        def _():
-            stage_corner(i + 1)
+        @pl.when(i + AHEAD < chunks)
+        def _():
+            stage_send(i + AHEAD)
+
+        @pl.when(i + CORNERS_AHEAD < chunks)
+        def _():
+            stage_corner(i + CORNERS_AHEAD)
 
         @pl.when(i < chunks)
         def _():
@@ -209,18 +271,31 @@
             stage_out(i - 2)
         return carry
 
-    stage_corner(0)
+    for c in range(CORNERS_AHEAD):
+        stage_corner(c)
+    for load in loads:
+        load.wait()
     lax.fori_loop(0, chunks + 2, step, 0)
 
     def finish(c, carry):
         y_kv(c).wait_send()
         y_part(c).wait_send()
-        for side in (0, 1):
-            @pl.when(has[side])
-            def _():
-                z_kv(side, c).wait_send()
+        sides(lambda side: z_kv(side, c).wait_send())
+
+        def ha_then_wa():
+            def sent(side):
                 z_corner(side, c).wait_send()
-                z_part(side, c).wait_send()
+                z_part(side, c, rows + 1).wait_send()
+            sides(sent)
+
+        def wa_then_ha():
+            def sent(side):
+                y_corner(side, c).wait_send()
+                corner_part(side, c).wait_send()
+                z_part(side, c, rows).wait_send()
+            sides(sent)
+
+        lax.cond(wa_first(c), wa_then_ha, ha_then_wa)
         out_q(c).wait()
         out_kv(c).wait()
         return carry
@@ -236,16 +311,20 @@
     width = HEADS_PER_CHUNK * HEAD_DIM
     assert channels % width == 0
     chunks = channels // width
-    assert chunks >= 2
+    assert chunks >= AHEAD >= CORNERS_AHEAD
     n_q = grid_t * rows * cols * tok
     n_k = n_q + grid_t * tok * (cols + 2 * (rows + 1))
-    vmem = pl.BlockSpec(memory_space=pltpu.VMEM)
+    stay = pl.BlockSpec(memory_space=pl.ANY)
     out = pl.pallas_call(
         functools.partial(kernel, (n_sec, n_ha, n_wa, chunks, width)),
         out_shape=jax.ShapeDtypeStruct((3,) + q.shape, BF16),
-        in_specs=[pl.BlockSpec(memory_space=pltpu.SMEM), vmem, vmem, vmem],
+        in_specs=[pl.BlockSpec(memory_space=pltpu.SMEM), stay, stay, stay],
         out_specs=pl.BlockSpec(memory_space=pl.ANY),
         scratch_shapes=[
+            pltpu.VMEM(q.shape, BF16),
+            pltpu.VMEM(kv.shape, BF16),
+            pltpu.VMEM(go.shape, BF16),
+            pltpu.SemaphoreType.DMA((3,)),
             pltpu.VMEM((2, grid_t, cols, tok, channels), BF16),
             pltpu.VMEM((2, 2, grid_t, rows + 1, tok, channels), BF16),
             pltpu.VMEM((2, 2, grid_t, rows + 1, tok, channels), BF16),
@@ -263,7 +342,7 @@
         compiler_params=pltpu.CompilerParams(
             collective_id=0, has_side_effects=True, vmem_limit_bytes=60 * 1024 * 1024
         ),
-    )(time_start, q, kv, go)
+    )(time_start.transpose(1, 2, 0), q, kv, go)
     return out[:, None]
 
 

time: 110 us -> 99.7 us (0.906)
  Pallas kernels: 104 us -> 95.1 us
  local copies, waits for them, and re-layouts: 5.77 us -> 4.42 us
    pallas_call x1, Pallas kernels: 104 us -> 95.1 us  [local(): pl.pallas_call(functools.partial(kernel, (n_sec, n_ha, n_wa, chunks, widt...]
    unnamed x2 -> x1, local copies, waits for them, and re-layouts: 5.77 us -> 4.42 us
where the time goes in v1:
time: 99.7 us; the launch traced here: 99.5 us
  Pallas kernels  95.1 us (95%)
  local copies, waits for them, and re-layouts  4.42 us (4%)
    pallas_call x1, Pallas kernels, local(): pl.pallas_call(functools.partial(kernel, (n_sec, n_ha, n_wa, chunks, widt...  95.1 us
    unnamed x1, local copies, waits for them, and re-layouts  4.42 us

profile of v1, /device:TPU:1, one launch (start us, length us, event | category | flops | bytes accessed | tf_op | source)
XLA Modules:
  0.0 99.5 jit_solution(17966377808013431889)
XLA Ops:
  0.0 95.1 %shard_map.46 = bf16[3,4,2,2,16,2560]{5,4,3,2,1,0:T(8,128)(2,1)} custom-call(s32[2,2,4]{2,1,0:T(2,128)} %bitcast.11, bf16[4,2,2,16,2560]{4,3,2,1,0:T(8,128)(2,1)} %bitcast.9, bf16[2,4,2,2,16,2560]{5,4,3,2,1,0:T(8,128)(2,1)} %bitcast.8, bf16[4,2,2,16,2560]{4,3,2,1,0:T(8,128)(2,1)} %bitcast.10), custom_call_target="tpu_custom_call" | custom-call | tf_op jit(solution)/shard_map/pallas_call | solution.py:318
  95.1 4.4 %copy.7 = bf16[3,1,4,2,2,16,2560]{6,5,4,3,2,1,0:T(8,128)(2,1)} copy(bf16[3,1,4,2,2,16,2560]{6,5,4,3,2,1,0:T(8,128)(2,1)} %bitcast.7) | data formatting | bytes 7864320

commit v2 on v1

--- a/solution.py
+++ b/solution.py
@@ -8,19 +8,21 @@
 from jax.sharding import PartitionSpec as P
 
 HEAD_DIM = 128
-HEADS_PER_CHUNK = 2
+HEADS_PER_CHUNK = 1
 MESH = pl.DeviceIdType.MESH
 F32 = jnp.float32
 BF16 = jnp.bfloat16
 
 Y_KV, Z_KV, CORNER, Z_PART, Y_PART, OUT_Q, OUT_KV, CORNER_PART, KINDS = 0, 1, 3, 5, 7, 8, 9, 10, 12
 
-AHEAD = 2
-CORNERS_AHEAD = 1
+AHEAD = 5
+CORNERS_AHEAD = 3
+FOLD_LAG = 3
+OUT_LAG = 6
 
 
 def wa_first(c):
-    return lax.rem(c, 3) == 2
+    return lax.rem(c, 3) == 1
 
 
 def dot(a, b, contract):
@@ -262,20 +264,20 @@
         def _():
             stage_compute(i)
 
-        @pl.when((i >= 1) & (i < chunks + 1))
-        def _():
-            stage_fold(i - 1)
-
-        @pl.when(i >= 2)
-        def _():
-            stage_out(i - 2)
+        @pl.when((i >= FOLD_LAG) & (i < chunks + FOLD_LAG))
+        def _():
+            stage_fold(i - FOLD_LAG)
+
+        @pl.when(i >= OUT_LAG)
+        def _():
+            stage_out(i - OUT_LAG)
         return carry
 
     for c in range(CORNERS_AHEAD):
         stage_corner(c)
     for load in loads:
         load.wait()
-    lax.fori_loop(0, chunks + 2, step, 0)
+    lax.fori_loop(0, chunks + OUT_LAG, step, 0)
 
     def finish(c, carry):
         y_kv(c).wait_send()
@@ -301,6 +303,19 @@
         return carry
 
     lax.fori_loop(0, chunks, finish, 0)
+
+
+def copy_kernel(src, dst, held, sems):
+    parts = [(i, t) for i in range(src.shape[0]) for t in range(src.shape[1])]
+    come = [pltpu.make_async_copy(src.at[p], held.at[p], sems.at[0, n]) for n, p in enumerate(parts)]
+    go = [pltpu.make_async_copy(held.at[p], dst.at[p], sems.at[1, n]) for n, p in enumerate(parts)]
+    for copy in come:
+        copy.start()
+    for a, b in zip(come, go):
+        a.wait()
+        b.start()
+    for copy in go:
+        copy.wait()
 
 
 def local(mesh_sizes, queries, keys_values, grad_out, time_start):
@@ -343,6 +358,13 @@
             collective_id=0, has_side_effects=True, vmem_limit_bytes=60 * 1024 * 1024
         ),
     )(time_start.transpose(1, 2, 0), q, kv, go)
+    out = pl.pallas_call(
+        copy_kernel,
+        out_shape=jax.ShapeDtypeStruct(out.shape, BF16),
+        in_specs=[pl.BlockSpec(memory_space=pl.ANY)],
+        out_specs=pl.BlockSpec(memory_space=pl.ANY),
+        scratch_shapes=[pltpu.VMEM(out.shape, BF16), pltpu.SemaphoreType.DMA((2, 3 * grid_t))],
+    )(out)
     return out[:, None]
 
 

time: 99.7 us -> 97.4 us (0.977)
  local copies, waits for them, and re-layouts: 4.42 us -> 0 us
  Pallas kernels: 95.1 us -> 97.3 us
    unnamed x1 -> x0, local copies, waits for them, and re-layouts: 4.42 us -> none
    pallas_call x0 -> x1, Pallas kernels: none -> 3.47 us  [local(): pl.pallas_call(copy_kernel, out_shape=jax.ShapeDtypeStruct(out.shape, BF1...]
    pallas_call x1, Pallas kernels: 95.1 us -> 93.8 us  [local(): pl.pallas_call(functools.partial(kernel, (n_sec, n_ha, n_wa, chunks, widt...]
where the time goes in v2:
time: 97.4 us; the launch traced here: 97.3 us
  Pallas kernels  97.3 us (100%)
    pallas_call x1, Pallas kernels, local(): pl.pallas_call(functools.partial(kernel, (n_sec, n_ha, n_wa, chunks, widt...  93.8 us
    pallas_call x1, Pallas kernels, local(): pl.pallas_call(copy_kernel, out_shape=jax.ShapeDtypeStruct(out.shape, BF1...  3.47 us

profile of v2, /device:TPU:1, one launch (start us, length us, event | category | flops | bytes accessed | tf_op | source)
XLA Modules:
  0.0 97.3 jit_solution(10149370705329952297)
XLA Ops:
  0.0 93.8 %shard_map.46.src = bf16[3,4,2,2,16,2560]{5,4,3,2,1,0:T(8,128)(2,1)} custom-call(s32[2,2,4]{2,1,0:T(2,128)} %bitcast.10, bf16[4,2,2,16,2560]{4,3,2,1,0:T(8,128)(2,1)} %bitcast.8, bf16[2,4,2,2,16,2560]{5,4,3,2,1,0:T(8,128)(2,1)} %bitcast.7, bf16[4,2,2,16,2560]{4,3,2,1,0:T(8,128)(2,1)} %bitcast.9), custom_call_target="tpu_custom_call" | custom-call | tf_op jit(solution)/shard_map/pallas_call | solution.py:333
  93.8 3.5 %shard_map.47 = bf16[3,4,2,2,16,2560]{5,4,3,2,1,0:T(8,128)(2,1)} custom-call(bf16[3,4,2,2,16,2560]{5,4,3,2,1,0:T(8,128)(2,1)} %shard_map.46.src), custom_call_target="tpu_custom_call" | custom-call | tf_op jit(solution)/shard_map/pallas_call | solution.py:361
